TPU v7x, 512 devices: a whole 4x4x16 slice. The times are simulated.
512 devices in a mesh: slab: 32 (over x, y, z_hi), tile: 16 (over z_lo, core).
Axes of the slice: x: 4, y: 4, z: 16 (z_hi: 2, z_lo: 8; z = z_hi * 8 + z_lo), core: 2. Of those that a mesh axis runs over, the one named last changes fastest.
Arguments:
- field: float32 [256, 256, 1024], P('slab', 'tile'), may hold values from -1 to 1
- dual: float32 [3, 256, 256, 1024], P(None, 'slab', 'tile'), may hold values from -0.5 to 0.5
- depth: float32 [32, 2, 4, 256, 1024], P('slab', None, None, 'tile'), may hold values from 0 to 256
- owner: int32 [2], replicated, may hold values from 0 to 31
- visible: int32 [2, 4, 16], P(None, None, 'tile'), may hold values 0 or 1
Outputs:
- field_out: float32 [256, 256, 1024], P('slab', 'tile')
- dual_out: float32 [3, 256, 256, 1024], P(None, 'slab', 'tile')
All inputs are finite; a program needn't handle non-finite values. No bound on the sum of `visible` on one device may be relied on, other than what follows from the above.
Results may differ from a plain program's by a relative error of at most 0.00002.
Values sent between devices are 32-bit elements; how exact they have to be, the bound alone decides.
No kernel may reach another device: no remote copies, remote signals or barrier semaphores. Data moves between devices by JAX's collectives and lax.ppermute only.
A program may use at most 64 MiB of HBM per device.

v0:
```python
import jax
import jax.numpy as jnp
from jax import lax
from jax.sharding import PartitionSpec as P

VIEWS = 4
BINS = 8
BAND = 6
ITERS = 2


def from_root(value, axis, root):
    mine = lax.axis_index(axis) == root
    return lax.psum(jnp.where(mine, value, jnp.zeros_like(value)), axis)


def passed_along(value, axis, steps):
    count = lax.axis_size(axis)
    first, last = (max(0, -steps), min(count, count - steps))
    return lax.ppermute(value, axis, [(source, source + steps) for source in range(first, last)])


def add_votes(histogram, depth_map, seen, zfloat):
    ratio = (depth_map[None, :, :] - zfloat) / float(BAND)
    weight = jnp.clip(ratio + 2.0, 0.0, 1.0) * seen
    place = (jnp.clip(ratio, -1.0, 1.0) + 1.0) * ((BINS - 1) / 2.0)
    return [
        histogram[bin_index] + weight * jnp.maximum(0.0, 1.0 - jnp.abs(place - float(bin_index)))
        for bin_index in range(BINS)
    ]


def proximal(values, histogram):
    total = histogram[0]
    for bin_index in range(1, BINS):
        total = total + histogram[bin_index]
    weights = -total
    best = jnp.minimum(values - 0.05 * weights, -1.0)
    weights = weights + 2.0 * histogram[0]
    for bin_index in range(1, BINS):
        centre = -1.0 + 2.0 * bin_index / (BINS - 1)
        best = jnp.maximum(best, jnp.minimum(values - 0.05 * weights, centre))
        weights = weights + 2.0 * histogram[bin_index]
    return jnp.maximum(best, values - 0.05 * weights)


def dual_step(
    dual_z, dual_x, dual_y, here, ahead_z, ahead_x, zpos, xpos, ypos, total_z, total_x, total_y
):
    zero_y = jnp.zeros(here.shape[:2] + (1,), jnp.float32)
    ahead_y = jnp.concatenate([here[:, :, 1:], zero_y], 2)
    grad_z = jnp.where(zpos < total_z - 1, ahead_z - here, 0.0)
    grad_x = jnp.where(xpos < total_x - 1, ahead_x - here, 0.0)
    grad_y = jnp.where(ypos < total_y - 1, ahead_y - here, 0.0)
    moved_z = dual_z + 0.25 * grad_z
    moved_x = dual_x + 0.25 * grad_x
    moved_y = dual_y + 0.25 * grad_y
    scale = jnp.maximum(1.0, jnp.sqrt(moved_z * moved_z + moved_x * moved_x + moved_y * moved_y))
    inside_z = (zpos >= 0) & (zpos < total_z - 1)
    inside_x = (xpos >= 0) & (xpos < total_x - 1)
    new_z = jnp.where(inside_z, moved_z / scale, 0.0)
    new_x = jnp.where(inside_x, moved_x / scale, 0.0)
    new_y = jnp.where(ypos < total_y - 1, moved_y / scale, 0.0)
    return (new_z, new_x, new_y)


def per_device(field, dual, depth, owner, visible):
    slab_cells, strip_cells, depth_cells = field.shape
    total_z = slab_cells * lax.axis_size("slab")
    total_x = strip_cells * lax.axis_size("tile")
    slab_start = lax.axis_index("slab") * slab_cells
    strip_start = lax.axis_index("tile") * strip_cells
    zpos = slab_start + jnp.arange(slab_cells, dtype=jnp.int32)[:, None, None]
    xpos = strip_start + jnp.arange(strip_cells, dtype=jnp.int32)[None, :, None]
    ypos = jnp.arange(depth_cells, dtype=jnp.int32)[None, None, :]
    zfloat = zpos.astype(jnp.float32)
    histogram = [jnp.zeros(field.shape, jnp.float32) for bin_index in range(BINS)]
    current = field
    dual_z, dual_x, dual_y = (dual[0], dual[1], dual[2])
    extra = field
    zero_y = jnp.zeros((slab_cells, strip_cells, 1), jnp.float32)
    for step_index in range(ITERS):
        batch = from_root(depth[0, step_index], "slab", owner[step_index])
        for view_index in range(VIEWS):
            seen = visible[step_index, view_index, 0].astype(jnp.float32)
            histogram = add_votes(histogram, batch[view_index], seen, zfloat)
        below = passed_along(extra[0:1], "slab", -1)
        beside = passed_along(extra[:, 0:1], "tile", -1)
        ahead_z = jnp.concatenate([extra[1:], below], 0)
        ahead_x = jnp.concatenate([extra[:, 1:], beside], 1)
        dual_z, dual_x, dual_y = dual_step(
            dual_z,
            dual_x,
            dual_y,
            extra,
            ahead_z,
            ahead_x,
            zpos,
            xpos,
            ypos,
            total_z,
            total_x,
            depth_cells,
        )
        above = passed_along(dual_z[-1:], "slab", 1)
        before = passed_along(dual_x[:, -1:], "tile", 1)
        prev_z = jnp.concatenate([above, dual_z[:-1]], 0)
        prev_x = jnp.concatenate([before, dual_x[:, :-1]], 1)
        prev_y = jnp.concatenate([zero_y, dual_y[:, :, :-1]], 2)
        divergence = dual_z - prev_z + (dual_x - prev_x) + (dual_y - prev_y)
        updated = proximal(current + 0.25 * divergence, histogram)
        extra = 2.0 * updated - current
        current = updated
    return (current, jnp.stack([dual_z, dual_x, dual_y]))


def solution(mesh):
    placed = (
        P("slab", "tile", None),
        P(None, "slab", "tile", None),
        P("slab", None, None, "tile", None),
        P(),
        P(None, None, "tile"),
    )
    return jax.shard_map(
        per_device,
        mesh=mesh,
        in_specs=placed,
        out_specs=(P("slab", "tile", None), P(None, "slab", "tile", None)),
        check_vma=False,
    )
```

profile of v0, /device:TPU:23, one launch (start us, length us, event | category | flops | bytes accessed | tf_op | source)
XLA Modules:
  0.0 672.6 jit_solution(14026309236746614929)
XLA Ops:
  7.2 0.0 copy-start
  7.2 0.0 copy-start.2
  7.2 0.0 all-reduce.7.cloned.1.call-start
  7.2 1.0 slice.134
  8.3 2.6 collective-permute-start.1
  10.8 0.8 slice.131
  11.7 15.3 %collective-permute-start = (f32[1,16,1024]{2,1,0:T(8,128)S(1)}, f32[1,16,1024]{2,1,0:T(8,128)S(1)}, u32[]{:S(2)}, u32[]{:S(2)}) collective-permute-start(f32[1,16,1024]{2,1,0:T(8,128)S(1)} %slice.131), channel_id=1, source_target_pairs={{16,0},{32,16},{48,32},{64,48},{80,64},{96,80},{112,96},{128,112},... | collective-permute-start | bytes 196616 | tf_op jit(solution)/shard_map/ppermute | solution.py:20
  27.0 1.3 fusion.28
  29.6 1.9 select_bitcast_fusion
  31.5 0.0 all-reduce.7.cloned.1.call-update
  31.5 0.0 slice-start
  31.6 0.0 copy-done.2
  31.6 0.7 fusion.27
  32.3 0.0 copy-done
  32.3 0.1 slice.133
  32.3 0.2 slice.136
  37.4 0.0 collective-permute-done.1
  37.4 0.0 collective-permute-done
  37.5 0.0 slice-done
  37.5 2.0 divide_select_fusion.3
  39.4 0.3 divide_select_fusion.5
  39.9 3.3 collective-permute-start.3
  43.1 9.4 %collective-permute-start.2 = (f32[1,16,1024]{2,1,0:T(8,128)S(1)}, f32[1,16,1024]{2,1,0:T(8,128)S(1)}, u32[]{:S(2)}, u32[]{:S(2)}) collective-permute-start(f32[1,16,1024]{2,1,0:T(8,128)S(1)} %slice.172), channel_id=1, source_target_pairs={{0,16},{16,32},{32,48},{48,64},{64,80},{80,96},{96,112},{112,128},... | collective-permute-start | bytes 196616 | tf_op jit(solution)/shard_map/ppermute | solution.py:20
  52.5 534.5 %all-reduce.7.cloned.1.call-done = (f32[4,16,1024]{2,1,0:T(8,128)}, f32[4,16,1024]{2,1,0:T(8,128)}) async-done(((f32[4,16,1024]{2,1,0:T(8,128)}, f32[4,16,1024]{2,1,0:T(8,128)}), (f32[4,16,1024]{2,1,0:T(8,128)}, f32[4,16,1024]{2,1,0:T(8,128)})) %all-reduce.7.cloned.1.call-update) | async-done | bytes 524304 | tf_op jit(solution)/shard_map/psum | solution.py:14
  587.0 1.0 slice_bitcast_fusion.7
  588.0 0.0 collective-permute-done.3
  588.0 0.0 collective-permute-done.2
  588.0 0.0 copy-start.1
  588.0 5.0 multiply_subtract_fusion
  593.1 24.7 %collective-permute-start.5 = (f32[8,1,1024]{2,1,0:T(1,128)S(1)}, f32[8,1,1024]{2,1,0:T(1,128)S(1)}, u32[]{:S(2)}, u32[]{:S(2)}) collective-permute-start(f32[8,1,1024]{2,1,0:T(1,128)S(1)} %slice.184), channel_id=1, source_target_pairs={{1,0},{2,1},{3,2},{4,3},{5,4},{6,5},{7,6},{8,7},{9,8},{10,9},{11,1... | collective-permute-start | bytes 98312 | tf_op jit(solution)/shard_map/ppermute | solution.py:20
  617.8 2.4 collective-permute-start.4
  620.2 0.0 copy-done.1
  620.3 0.2 slice.185
  620.5 0.1 slice.183
  620.5 0.0 collective-permute-done.5
  620.6 12.3 %collective-permute-done.4 = f32[1,16,1024]{2,1,0:T(8,128)S(1)} collective-permute-done((f32[1,16,1024]{2,1,0:T(8,128)S(1)}, f32[1,16,1024]{2,1,0:T(8,128)S(1)}, u32[]{:S(2)}, u32[]{:S(2)}) %collective-permute-start.4) | collective-permute-done | bytes 65568 | tf_op jit(solution)/shard_map/ppermute | solution.py:20
  632.9 0.6 divide_select_fusion
  633.4 0.2 divide_select_fusion.2
  633.7 3.1 collective-permute-start.7
  636.8 10.0 %collective-permute-start.6 = (f32[1,16,1024]{2,1,0:T(8,128)S(1)}, f32[1,16,1024]{2,1,0:T(8,128)S(1)}, u32[]{:S(2)}, u32[]{:S(2)}) collective-permute-start(f32[1,16,1024]{2,1,0:T(8,128)S(1)} %slice.186), channel_id=1, source_target_pairs={{0,16},{16,32},{32,48},{48,64},{64,80},{80,96},{96,112},{112,128},... | collective-permute-start | bytes 196616 | tf_op jit(solution)/shard_map/ppermute | solution.py:20
  646.8 1.2 pad_maximum_fusion
  648.1 0.0 collective-permute-done.7
  648.1 8.1 %collective-permute-done.6 = f32[1,16,1024]{2,1,0:T(8,128)S(1)} collective-permute-done((f32[1,16,1024]{2,1,0:T(8,128)S(1)}, f32[1,16,1024]{2,1,0:T(8,128)S(1)}, u32[]{:S(2)}, u32[]{:S(2)}) %collective-permute-start.6) | collective-permute-done | bytes 65568 | tf_op jit(solution)/shard_map/ppermute | solution.py:20
  656.2 9.6 %subtract_maximum_fusion = f32[8,16,1024]{2,1,0:T(8,128)} fusion(f32[8,16,1024]{2,1,0:T(8,128)S(1)} %get-tuple-element.9, f32[8,16,1024]{2,1,0:T(8,128)S(1)} %get-tuple-element.17, f32[8,15,1024]{2,1,0:T(8,128)S(1)} %bitcast.48, f32[8,1,1024]{2,1,0:T(1,128)S(1)} %collective-permute-done.7, f32[8,16,1024]{2,1,0:T(8,128)S(1)} %get-tuple-element.16, ...), kind=kLoop, calls=%fused_computation.30 | loop fusion | flops 65404928 | bytes 4718144 | tf_op jit(solution)/shard_map/max | solution.py:44
  (14 shorter events, 0.2 us)
Async XLA Ops:
  7.2 25.1 %copy-start = (f32[8,16,1024]{2,1,0:T(8,128)S(1)}, f32[8,16,1024]{2,1,0:T(8,128)}, u32[]{:S(2)}) copy-start(f32[8,16,1024]{2,1,0:T(8,128)} %param.5) | copy-start | bytes 1572868
  7.2 24.4 %copy-start.2 = (s32[2,4,1]{1,2,0:T(1,128)S(1)}, s32[2,4,1]{1,2,0:T(1,128)}, u32[]{:S(2)}) copy-start(s32[2,4,1]{1,2,0:T(1,128)} %param.9) | copy-start | bytes 100
  7.2 579.8 %all-reduce.7.cloned.1.call-start = ((), (), s32[]{:S(2)}) async-start(), calls=%async_computation | async-start | bytes 1048576 | tf_op jit(solution)/shard_map/psum | solution.py:14
  8.3 29.2 %collective-permute-start.1 = (f32[8,1,1024]{2,1,0:T(1,128)S(1)}, f32[8,1,1024]{2,1,0:T(1,128)S(1)}, u32[]{:S(2)}, u32[]{:S(2)}) collective-permute-start(f32[8,1,1024]{2,1,0:T(1,128)S(1)} %slice.134), channel_id=1, source_target_pairs={{1,0},{2,1},{3,2},{4,3},{5,4},{6,5},{7,6},{8,7},{9,8},{10,9},{11,1... | collective-permute-start | bytes 98312 | tf_op jit(solution)/shard_map/ppermute | solution.py:20
  11.7 25.8 %collective-permute-start = (f32[1,16,1024]{2,1,0:T(8,128)S(1)}, f32[1,16,1024]{2,1,0:T(8,128)S(1)}, u32[]{:S(2)}, u32[]{:S(2)}) collective-permute-start(f32[1,16,1024]{2,1,0:T(8,128)S(1)} %slice.131), channel_id=1, source_target_pairs={{16,0},{32,16},{48,32},{64,48},{80,64},{96,80},{112,96},{128,112},... | collective-permute-start | bytes 196616 | tf_op jit(solution)/shard_map/ppermute | solution.py:20
  31.5 5.9 slice-start
  39.9 548.1 %collective-permute-start.3 = (f32[8,1,1024]{2,1,0:T(1,128)S(1)}, f32[8,1,1024]{2,1,0:T(1,128)S(1)}, u32[]{:S(2)}, u32[]{:S(2)}) collective-permute-start(f32[8,1,1024]{2,1,0:T(1,128)S(1)} %slice.174), channel_id=1, source_target_pairs={{0,1},{1,2},{2,3},{3,4},{4,5},{5,6},{6,7},{7,8},{8,9},{9,10},{10,1... | collective-permute-start | bytes 98312 | tf_op jit(solution)/shard_map/ppermute | solution.py:20
  43.1 544.8 %collective-permute-start.2 = (f32[1,16,1024]{2,1,0:T(8,128)S(1)}, f32[1,16,1024]{2,1,0:T(8,128)S(1)}, u32[]{:S(2)}, u32[]{:S(2)}) collective-permute-start(f32[1,16,1024]{2,1,0:T(8,128)S(1)} %slice.172), channel_id=1, source_target_pairs={{0,16},{16,32},{32,48},{48,64},{64,80},{80,96},{96,112},{112,128},... | collective-permute-start | bytes 196616 | tf_op jit(solution)/shard_map/ppermute | solution.py:20
  588.0 32.2 %copy-start.1 = (f32[4,16,1024]{2,1,0:T(8,128)S(1)}, f32[4,16,1024]{2,1,0:T(8,128)}, u32[]{:S(2)}) copy-start(f32[4,16,1024]{2,1,0:T(8,128)} %get-tuple-element.3) | copy-start | bytes 786436
  593.1 27.5 %collective-permute-start.5 = (f32[8,1,1024]{2,1,0:T(1,128)S(1)}, f32[8,1,1024]{2,1,0:T(1,128)S(1)}, u32[]{:S(2)}, u32[]{:S(2)}) collective-permute-start(f32[8,1,1024]{2,1,0:T(1,128)S(1)} %slice.184), channel_id=1, source_target_pairs={{1,0},{2,1},{3,2},{4,3},{5,4},{6,5},{7,6},{8,7},{9,8},{10,9},{11,1... | collective-permute-start | bytes 98312 | tf_op jit(solution)/shard_map/ppermute | solution.py:20
  617.8 15.1 %collective-permute-start.4 = (f32[1,16,1024]{2,1,0:T(8,128)S(1)}, f32[1,16,1024]{2,1,0:T(8,128)S(1)}, u32[]{:S(2)}, u32[]{:S(2)}) collective-permute-start(f32[1,16,1024]{2,1,0:T(8,128)S(1)} %slice.182), channel_id=1, source_target_pairs={{16,0},{32,16},{48,32},{64,48},{80,64},{96,80},{112,96},{128,112},... | collective-permute-start | bytes 196616 | tf_op jit(solution)/shard_map/ppermute | solution.py:20
  633.7 14.4 %collective-permute-start.7 = (f32[8,1,1024]{2,1,0:T(1,128)S(1)}, f32[8,1,1024]{2,1,0:T(1,128)S(1)}, u32[]{:S(2)}, u32[]{:S(2)}) collective-permute-start(f32[8,1,1024]{2,1,0:T(1,128)S(1)} %slice.188), channel_id=1, source_target_pairs={{0,1},{1,2},{2,3},{3,4},{4,5},{5,6},{6,7},{7,8},{8,9},{9,10},{10,1... | collective-permute-start | bytes 98312 | tf_op jit(solution)/shard_map/ppermute | solution.py:20
  636.8 19.4 %collective-permute-start.6 = (f32[1,16,1024]{2,1,0:T(8,128)S(1)}, f32[1,16,1024]{2,1,0:T(8,128)S(1)}, u32[]{:S(2)}, u32[]{:S(2)}) collective-permute-start(f32[1,16,1024]{2,1,0:T(8,128)S(1)} %slice.186), channel_id=1, source_target_pairs={{0,16},{16,32},{32,48},{48,64},{64,80},{80,96},{96,112},{112,128},... | collective-permute-start | bytes 196616 | tf_op jit(solution)/shard_map/ppermute | solution.py:20
Sparse Core Ops, SparseCore 0:
  31.7 555.2 all-reduce.6
where the time goes:
time: 673 us
  waiting for transfers between devices  555 us (82%)
  starting transfers between devices  70.7 us (11%)
  other arithmetic  20.8 us (3%)
  between operations  20.5 us (3%)
    psum x1, waiting for transfers between devices, from_root(): return lax.psum(jnp.where(mine, value, jnp.zeros_like(value)), axis)  535 us
    ppermute x8, starting transfers between devices, passed_along(): lax.ppermute(value, axis, [(source, source + steps) for source in range(f...  70.7 us
    ppermute x8, waiting for transfers between devices, passed_along(): lax.ppermute(value, axis, [(source, source + steps) for source in range(f...  20.4 us
  transfers between devices with their start and end apart: 9, of which 3 were waited for; matrix products, arithmetic and copies ran while one was open for 1% of the time, Pallas kernels for 0%

commit v1 on v0

--- a/solution.py
+++ b/solution.py
@@ -11,7 +11,7 @@
 
 def from_root(value, axis, root):
     mine = lax.axis_index(axis) == root
-    return lax.psum(jnp.where(mine, value, jnp.zeros_like(value)), axis)
+    return jnp.sum(lax.all_gather(jnp.where(mine, value, jnp.zeros_like(value)), axis), axis=0)
 
 
 def passed_along(value, axis, steps):

time: 673 us -> 566 us (0.84)
  the two profiles are of different devices: /device:TPU:23 before, /device:TPU:67 now
where the time goes in v1:
time: 566 us
  waiting for transfers between devices  462 us (82%)
  starting transfers between devices  50 us (9%)
  other arithmetic  29.8 us (5%)
  between operations  20.5 us (4%)
    all_gather x2, waiting for transfers between devices, from_root(): lax.all_gather(jnp.where(mine, value, jnp.zeros_like(value)), axis)  444 us
    ppermute x8, starting transfers between devices, passed_along(): lax.ppermute(value, axis, [(source, source + steps) for source in range(f...  49.9 us
    ppermute x8, waiting for transfers between devices, passed_along(): lax.ppermute(value, axis, [(source, source + steps) for source in range(f...  16.6 us
  transfers between devices with their start and end apart: 10, of which 4 were waited for; matrix products, arithmetic and copies ran while one was open for 3% of the time, Pallas kernels for 0%

profile of v1, /device:TPU:67, one launch (start us, length us, event | category | flops | bytes accessed | tf_op | source)
XLA Modules:
  0.0 565.6 jit_solution(10060643121510752463)
XLA Ops:
  7.2 0.0 copy-start
  7.2 0.0 copy-start.1
  7.2 0.0 all-gather.5.cloned.1.call-start
  7.2 1.3 fusion.28
  9.9 1.9 slice_select_fusion
  11.7 0.0 all-gather.5.cloned.1.call-update
  11.8 0.0 all-gather.7.cloned.1.call-start
  11.8 0.7 all-gather.7.cloned.1.call-update
  12.5 0.0 copy-done
  12.6 0.0 slice-start
  12.6 2.7 collective-permute-start.1
  15.3 16.1 %collective-permute-start = (f32[1,16,1024]{2,1,0:T(8,128)S(1)}, f32[1,16,1024]{2,1,0:T(8,128)S(1)}, u32[]{:S(2)}, u32[]{:S(2)}) collective-permute-start(f32[1,16,1024]{2,1,0:T(8,128)S(1)} %slice.131), channel_id=1, source_target_pairs={{16,0},{32,16},{48,32},{64,48},{80,64},{96,80},{112,96},{128,112},... | collective-permute-start | bytes 196616 | tf_op jit(solution)/shard_map/ppermute | solution.py:20
  31.4 0.0 copy-done.1
  31.4 0.7 fusion.27
  32.1 0.1 slice.133
  32.2 0.2 slice.136
  37.2 0.0 collective-permute-done.1
  37.2 1.5 collective-permute-done
  38.7 0.0 slice-done
  38.7 2.0 divide_select_fusion.3
  40.7 0.3 divide_select_fusion.5
  41.0 0.8 slice.173
  41.8 1.9 collective-permute-start.3
  43.8 10.1 %collective-permute-start.2 = (f32[1,16,1024]{2,1,0:T(8,128)S(1)}, f32[1,16,1024]{2,1,0:T(8,128)S(1)}, u32[]{:S(2)}, u32[]{:S(2)}) collective-permute-start(f32[1,16,1024]{2,1,0:T(8,128)S(1)} %slice.172), channel_id=1, source_target_pairs={{0,16},{16,32},{32,48},{48,64},{64,80},{80,96},{96,112},{112,128},... | collective-permute-start | bytes 196616 | tf_op jit(solution)/shard_map/ppermute | solution.py:20
  53.8 211.3 %all-gather.5.cloned.1.call-done = f32[32,1,4,16,1024]{4,3,2,1,0:T(8,128)} async-done(((f32[1,1,4,16,1024]{4,3,2,1,0:T(8,128)}), f32[32,1,4,16,1024]{4,3,2,1,0:T(8,128)}) %all-gather.5.cloned.1.call-update) | async-done | bytes 8388624 | tf_op jit(solution)/shard_map/all_gather | solution.py:14
  265.2 4.0 reduce_sum.18
  269.2 0.0 collective-permute-done.3
  269.2 0.0 collective-permute-done.2
  269.2 6.0 %multiply_subtract_fusion = (f32[8,16,1024]{2,1,0:T(8,128)S(1)}, f32[8,16,1024]{2,1,0:T(8,128)S(1)}) fusion(f32[8,16,1024]{2,1,0:T(8,128)S(1)} %copy-done, f32[]{:T(128)} %bitcast.11, f32[16,1024]{1,0:T(8,128)S(1)} %get-tuple-element.23, f32[]{:T(128)} %bitcast.9, f32[16,1024]{1,0:T(8,128)S(1)} %get-tuple-element.24, f32[]{:T(128)} %bitcast.7, ...), kind=kLoop, calls=%fused_computation.36 | loop fusion | flops 36831232 | bytes 4980272 | tf_op jit(solution)/shard_map/sub | solution.py:112
  275.2 3.0 collective-permute-start.5
  278.3 6.0 %collective-permute-start.4 = (f32[1,16,1024]{2,1,0:T(8,128)S(1)}, f32[1,16,1024]{2,1,0:T(8,128)S(1)}, u32[]{:S(2)}, u32[]{:S(2)}) collective-permute-start(f32[1,16,1024]{2,1,0:T(8,128)S(1)} %slice.182), channel_id=1, source_target_pairs={{16,0},{32,16},{48,32},{64,48},{80,64},{96,80},{112,96},{128,112},... | collective-permute-start | bytes 196616 | tf_op jit(solution)/shard_map/ppermute | solution.py:20
  284.2 233.1 %all-gather.7.cloned.1.call-done = f32[32,1,4,16,1024]{4,3,2,1,0:T(8,128)} async-done(((f32[1,1,4,16,1024]{4,3,2,1,0:T(8,128)}), f32[32,1,4,16,1024]{4,3,2,1,0:T(8,128)}) %all-gather.7.cloned.1.call-update) | async-done | bytes 8388624 | tf_op jit(solution)/shard_map/all_gather | solution.py:14
  517.4 4.0 reduce_sum.19
  521.4 0.2 slice.185
  521.6 0.1 slice.183
  521.7 0.0 collective-permute-done.5
  521.7 0.0 collective-permute-done.4
  521.7 0.6 divide_select_fusion
  522.3 0.2 divide_select_fusion.2
  522.6 8.3 %collective-permute-start.7 = (f32[8,1,1024]{2,1,0:T(1,128)S(1)}, f32[8,1,1024]{2,1,0:T(1,128)S(1)}, u32[]{:S(2)}, u32[]{:S(2)}) collective-permute-start(f32[8,1,1024]{2,1,0:T(1,128)S(1)} %slice.188), channel_id=1, source_target_pairs={{0,1},{1,2},{2,3},{3,4},{4,5},{5,6},{6,7},{7,8},{8,9},{9,10},{10,1... | collective-permute-start | bytes 98312 | tf_op jit(solution)/shard_map/ppermute | solution.py:20
  530.9 1.9 collective-permute-start.6
  532.8 1.2 pad_maximum_fusion
  534.1 0.0 collective-permute-done.7
  534.1 15.1 %collective-permute-done.6 = f32[1,16,1024]{2,1,0:T(8,128)S(1)} collective-permute-done((f32[1,16,1024]{2,1,0:T(8,128)S(1)}, f32[1,16,1024]{2,1,0:T(8,128)S(1)}, u32[]{:S(2)}, u32[]{:S(2)}) %collective-permute-start.6) | collective-permute-done | bytes 65568 | tf_op jit(solution)/shard_map/ppermute | solution.py:20
  549.2 9.6 %subtract_maximum_fusion = f32[8,16,1024]{2,1,0:T(8,128)} fusion(f32[8,16,1024]{2,1,0:T(8,128)S(1)} %get-tuple-element.7, f32[8,16,1024]{2,1,0:T(8,128)S(1)} %get-tuple-element.17, f32[8,15,1024]{2,1,0:T(8,128)S(1)} %bitcast.44, f32[8,1,1024]{2,1,0:T(1,128)S(1)} %collective-permute-done.7, f32[8,16,1024]{2,1,0:T(8,128)S(1)} %get-tuple-element.16, ...), kind=kLoop, calls=%fused_computation.30 | loop fusion | flops 65404928 | bytes 4718144 | tf_op jit(solution)/shard_map/max | solution.py:44
  (16 shorter events, 0.3 us)
Async XLA Ops:
  7.2 5.4 copy-start
  7.2 24.3 %copy-start.1 = (s32[2,4,1]{1,2,0:T(1,128)S(1)}, s32[2,4,1]{1,2,0:T(1,128)}, u32[]{:S(2)}) copy-start(s32[2,4,1]{1,2,0:T(1,128)} %param.9) | copy-start | bytes 100
  7.2 258.0 %all-gather.5.cloned.1.call-start = ((), (), s32[]{:S(2)}) async-start(), calls=%async_computation | async-start | bytes 8650752 | tf_op jit(solution)/shard_map/all_gather | solution.py:14
  11.8 505.6 %all-gather.7.cloned.1.call-start = ((), (), s32[]{:S(2)}) async-start(), calls=%async_computation.1 | async-start | bytes 8650752 | tf_op jit(solution)/shard_map/all_gather | solution.py:14
  12.6 26.1 %slice-start = ((f32[8,16,1024]{2,1,0:T(8,128)}), f32[7,16,1024]{2,1,0:T(8,128)S(1)}, s32[]{:S(2)}) async-start(f32[8,16,1024]{2,1,0:T(8,128)} %param.5), calls=%async_computation.2 | async-start | bytes 917504 | tf_op jit(solution)/shard_map/slice | solution.py:89
  12.6 24.6 %collective-permute-start.1 = (f32[8,1,1024]{2,1,0:T(1,128)S(1)}, f32[8,1,1024]{2,1,0:T(1,128)S(1)}, u32[]{:S(2)}, u32[]{:S(2)}) collective-permute-start(f32[8,1,1024]{2,1,0:T(1,128)S(1)} %slice.134), channel_id=1, source_target_pairs={{1,0},{2,1},{3,2},{4,3},{5,4},{6,5},{7,6},{8,7},{9,8},{10,9},{11,1... | collective-permute-start | bytes 98312 | tf_op jit(solution)/shard_map/ppermute | solution.py:20
  15.3 23.4 %collective-permute-start = (f32[1,16,1024]{2,1,0:T(8,128)S(1)}, f32[1,16,1024]{2,1,0:T(8,128)S(1)}, u32[]{:S(2)}, u32[]{:S(2)}) collective-permute-start(f32[1,16,1024]{2,1,0:T(8,128)S(1)} %slice.131), channel_id=1, source_target_pairs={{16,0},{32,16},{48,32},{64,48},{80,64},{96,80},{112,96},{128,112},... | collective-permute-start | bytes 196616 | tf_op jit(solution)/shard_map/ppermute | solution.py:20
  41.8 227.3 %collective-permute-start.3 = (f32[8,1,1024]{2,1,0:T(1,128)S(1)}, f32[8,1,1024]{2,1,0:T(1,128)S(1)}, u32[]{:S(2)}, u32[]{:S(2)}) collective-permute-start(f32[8,1,1024]{2,1,0:T(1,128)S(1)} %slice.174), channel_id=1, source_target_pairs={{0,1},{1,2},{2,3},{3,4},{4,5},{5,6},{6,7},{7,8},{8,9},{9,10},{10,1... | collective-permute-start | bytes 98312 | tf_op jit(solution)/shard_map/ppermute | solution.py:20
  43.8 225.4 %collective-permute-start.2 = (f32[1,16,1024]{2,1,0:T(8,128)S(1)}, f32[1,16,1024]{2,1,0:T(8,128)S(1)}, u32[]{:S(2)}, u32[]{:S(2)}) collective-permute-start(f32[1,16,1024]{2,1,0:T(8,128)S(1)} %slice.172), channel_id=1, source_target_pairs={{0,16},{16,32},{32,48},{48,64},{64,80},{80,96},{96,112},{112,128},... | collective-permute-start | bytes 196616 | tf_op jit(solution)/shard_map/ppermute | solution.py:20
  275.2 246.5 %collective-permute-start.5 = (f32[8,1,1024]{2,1,0:T(1,128)S(1)}, f32[8,1,1024]{2,1,0:T(1,128)S(1)}, u32[]{:S(2)}, u32[]{:S(2)}) collective-permute-start(f32[8,1,1024]{2,1,0:T(1,128)S(1)} %slice.184), channel_id=1, source_target_pairs={{1,0},{2,1},{3,2},{4,3},{5,4},{6,5},{7,6},{8,7},{9,8},{10,9},{11,1... | collective-permute-start | bytes 98312 | tf_op jit(solution)/shard_map/ppermute | solution.py:20
  278.3 243.4 %collective-permute-start.4 = (f32[1,16,1024]{2,1,0:T(8,128)S(1)}, f32[1,16,1024]{2,1,0:T(8,128)S(1)}, u32[]{:S(2)}, u32[]{:S(2)}) collective-permute-start(f32[1,16,1024]{2,1,0:T(8,128)S(1)} %slice.182), channel_id=1, source_target_pairs={{16,0},{32,16},{48,32},{64,48},{80,64},{96,80},{112,96},{128,112},... | collective-permute-start | bytes 196616 | tf_op jit(solution)/shard_map/ppermute | solution.py:20
  522.6 11.5 %collective-permute-start.7 = (f32[8,1,1024]{2,1,0:T(1,128)S(1)}, f32[8,1,1024]{2,1,0:T(1,128)S(1)}, u32[]{:S(2)}, u32[]{:S(2)}) collective-permute-start(f32[8,1,1024]{2,1,0:T(1,128)S(1)} %slice.188), channel_id=1, source_target_pairs={{0,1},{1,2},{2,3},{3,4},{4,5},{5,6},{6,7},{7,8},{8,9},{9,10},{10,1... | collective-permute-start | bytes 98312 | tf_op jit(solution)/shard_map/ppermute | solution.py:20
  530.9 18.3 %collective-permute-start.6 = (f32[1,16,1024]{2,1,0:T(8,128)S(1)}, f32[1,16,1024]{2,1,0:T(8,128)S(1)}, u32[]{:S(2)}, u32[]{:S(2)}) collective-permute-start(f32[1,16,1024]{2,1,0:T(8,128)S(1)} %slice.186), channel_id=1, source_target_pairs={{0,16},{16,32},{32,48},{48,64},{64,80},{80,96},{96,112},{112,128},... | collective-permute-start | bytes 196616 | tf_op jit(solution)/shard_map/ppermute | solution.py:20
Sparse Core Ops, SparseCore 0:
  12.3 252.7 all-gather.4
  270.0 247.2 all-gather.6
